TPU v7x, 768 devices: a whole 4x8x12 slice. The times are simulated.
768 devices in a mesh: grp: 48 (over y, z_lo, core), dp: 16 (over z_hi, x).
Axes of the slice: x: 4, y: 8, z: 12 (z_hi: 4, z_lo: 3; z = z_hi * 3 + z_lo), core: 2. Of those that a mesh axis runs over, the one named last changes fastest.
Arguments:
- vis_features: bfloat16 [49152, 3200], P(('grp', 'dp')), may hold values from -6 to 6
- vis_gain: float32 [3200], replicated, may hold values from 0.1 to 1.9
- proj_weight: bfloat16 [3200, 8192], P(None, 'dp'), may hold values from -0.109375 to 0.109375
- proj_bias: float32 [8192], P('dp'), may hold values from -3 to 3
- text_embed: bfloat16 [73728, 8192], P('grp', 'dp'), may hold values from -6 to 6
- out_gain: float32 [8192], P('dp'), may hold values from 0.1 to 1.9
- image_counts: int32 [768], P(('grp', 'dp')), may hold values from 1 to 4, as said below
- owner_block: int32 [3072], P(('grp', 'dp')), may hold values from 0 to 47, as said below
- offsets: int32 [3072], P(('grp', 'dp')), may hold values from 0 to 1520, as said below
Outputs:
- hidden: bfloat16 [73728, 8192], P('grp', 'dp')
Inputs may be any that keep to these rules, and one draw needn't show every extreme that they name: The live images of a device are its first image_counts slots; some device holds 4 in every draw. `owner_block`: among the image slots of one index of grp (live or not), at most 2 name the same owner, and in every such block some owner is named by exactly 2. `offsets`: the image slots that name one owner (live or not) cover disjoint runs of 16 positions inside its 1536 positions.
All inputs are finite; a program needn't handle non-finite values.
Results may differ from a plain program's by a relative error of at most 0.0043.
Values may be sent and summed in bfloat16 or wider, within the bound.
A program may use at most 64 MiB of HBM per device.

v0:
```python
import jax
import jax.numpy as jnp
from jax import lax
from jax.sharding import PartitionSpec as P

D = 8192


def on_device(
    vis_features,
    vis_gain,
    proj_weight,
    proj_bias,
    text_embed,
    out_gain,
    image_counts,
    owner_block,
    offsets,
):
    groups = lax.axis_size("grp")
    slots_device = owner_block.shape[0]
    per_image = vis_features.shape[0] // slots_device
    columns = proj_weight.shape[1]
    seq_len = text_embed.shape[0]
    capacity = seq_len // (groups * per_image)
    features_f = vis_features.astype(jnp.float32)
    normed = (
        features_f
        * lax.rsqrt(jnp.mean(features_f * features_f, axis=-1, keepdims=True) + 1e-06)
        * vis_gain
    ).astype(jnp.bfloat16)
    slot_local = jnp.arange(slots_device, dtype=jnp.int32)
    live_offsets = jnp.where(slot_local < image_counts[0], offsets, -1)
    block_owner, block_offsets = (
        lax.all_gather(owner_block, "dp", axis=0, tiled=True),
        lax.all_gather(live_offsets, "dp", axis=0, tiled=True),
    )
    projected = (
        jnp.dot(
            lax.all_gather(normed, "dp", axis=0, tiled=True),
            proj_weight,
            preferred_element_type=jnp.float32,
        )
        + proj_bias
    ).astype(jnp.bfloat16)
    block_slots = block_owner.shape[0]
    earlier = jnp.arange(block_slots)[:, None] > jnp.arange(block_slots)[None, :]
    same_owner = block_owner[:, None] == block_owner[None, :]
    rank_in = jnp.sum(same_owner & earlier, axis=1)
    bucket = block_owner * capacity + rank_in
    selector = jnp.arange(groups * capacity, dtype=jnp.int32)[:, None] == bucket[None, :]
    flat_rows = projected.reshape(block_slots, per_image * columns)
    bucketed = jnp.dot(
        selector.astype(jnp.bfloat16), flat_rows, preferred_element_type=jnp.float32
    ).astype(jnp.bfloat16)
    bucketed = bucketed.reshape(groups, capacity * per_image * columns)
    bucket_offsets = jnp.max(jnp.where(selector, block_offsets[None, :], -1), axis=1).reshape(
        groups, capacity
    )
    arrived, arrived_offsets = (
        lax.all_to_all(bucketed, "grp", split_axis=0, concat_axis=0, tiled=True),
        lax.all_to_all(bucket_offsets, "grp", split_axis=0, concat_axis=0, tiled=True),
    )
    received = arrived.reshape(groups * capacity * per_image, columns)
    starts = arrived_offsets.reshape(groups * capacity)
    target = jnp.where(
        starts[:, None] >= 0,
        starts[:, None] + jnp.arange(per_image, dtype=jnp.int32)[None, :],
        seq_len,
    )
    target = target.reshape(-1).astype(jnp.int32)
    merged = text_embed.at[target].set(received, mode="drop")
    local_squares = jnp.sum(jnp.square(merged.astype(jnp.float32)), axis=1)
    row_total = lax.psum(local_squares, "dp")
    inverse_rms = lax.rsqrt(row_total / D + 1e-05)
    hidden = merged.astype(jnp.float32) * inverse_rms[:, None] * out_gain
    return hidden.astype(jnp.bfloat16)


def solution(mesh):
    return jax.shard_map(
        on_device,
        mesh=mesh,
        in_specs=(
            P(("grp", "dp"), None),
            P(),
            P(None, "dp"),
            P("dp"),
            P("grp", "dp"),
            P("dp"),
            P(("grp", "dp")),
            P(("grp", "dp")),
            P(("grp", "dp")),
        ),
        out_specs=P("grp", "dp"),
        check_vma=False,
    )
```

profile of v0, /device:TPU:8, one launch (start us, length us, event | category | flops | bytes accessed | tf_op | source)
XLA Modules:
  0.0 344.0 jit_solution(8775235007260226890)
XLA Ops:
  6.6 2.8 copy.21
  9.6 0.9 fusion.5
  11.2 1.3 dynamic-slice
  13.5 29.4 %all-reduce.2 = (s32[64]{0:T(128)S(1)}, s32[64]{0:T(128)S(1)}) all-reduce(s32[64]{0:T(128)S(1)} %fusion.9, s32[64]{0:T(128)S(1)} %dynamic-update-slice), channel_id=1, replica_groups=mesh['grp'=48,'dp'=16] {'dp'}, use_global_device_ids=true, to_apply=%add.1 | all-reduce | flops 128 | bytes 1024
  43.2 0.7 all_to_all.12
  43.9 8.4 %all-to-all-start = ((s32[48,1,2]{2,1,0:T(1,128)}), s32[48,1,2]{2,1,0:T(1,128)S(1)}, u32[]{:S(2)}, u32[]{:S(2)}) async-start(s32[48,1,2]{2,1,0:T(1,128)} %bitcast.2), calls=%async_computation | async-start | bytes 49152 | tf_op jit(solution)/shard_map/all_to_all | solution.py:62
  52.4 98.1 %all-gather.2.cloned.1.call-done = bf16[1024,3200]{1,0:T(8,128)(2,1)} async-done(((bf16[64,3200]{1,0:T(8,128)(2,1)}), bf16[1024,3200]{1,0:T(8,128)(2,1)}) %all-gather.2.cloned.1.call-update) | async-done | bytes 6553616 | tf_op jit(solution)/shard_map/all_gather | solution.py:40
  150.5 7.5 %add_convert_fusion = bf16[1024,512]{1,0:T(8,128)(2,1)} fusion(bf16[1024,3200]{1,0:T(8,128)(2,1)} %all-gather.2.cloned.1.call-done, bf16[3200,512]{1,0:T(8,128)(2,1)S(1)} %copy-done, f32[512]{0:T(512)S(1)} %copy-done.5), kind=kOutput, calls=%fused_computation.7 | convolution fusion | flops 3356491776 | bytes 10881024 | tf_op jit(solution)/shard_map/dot_general | solution.py:39
  158.0 2.3 reshape.84
  160.3 3.0 convolution_convert_fusion
  163.4 8.6 %all_to_all.16 = bf16[48,1,16384]{2,1,0:T(2,128)(2,1)} reshape(bf16[96,8192]{1,0:T(8,128)(2,1)} %convolution_convert_fusion) | data formatting | bytes 3145728 | tf_op jit(solution)/shard_map/all_to_all | solution.py:61
  172.4 13.0 %reduce.7 = bf16[48,16384]{1,0:T(8,128)(2,1)} reduce(bf16[48,1,16384]{2,1,0:T(2,128)(2,1)} %all_to_all.16, bf16[]{:T(256)} %broadcast.60), dimensions={1}, to_apply=%all_to_all.16.reduce_sub_computation | reduce | bytes 3145730 | tf_op jit(solution)/shard_map/all_to_all | solution.py:61
  185.4 3.9 %reshape.115 = bf16[48,2,8192]{2,1,0:T(2,128)(2,1)} reshape(bf16[48,16384]{1,0:T(8,128)(2,1)} %reduce.7) | data formatting | bytes 3145728
  189.3 22.8 %all-to-all-start.1 = ((bf16[48,2,8192]{2,1,0:T(2,128)(2,1)}), bf16[48,2,8192]{2,1,0:T(2,128)(2,1)}, u32[]{:S(2)}, u32[]{:S(2)}) async-start(bf16[48,2,8192]{2,1,0:T(2,128)(2,1)} %reshape.115), calls=%async_computation.1 | async-start | bytes 3145728 | tf_op jit(solution)/shard_map/all_to_all | solution.py:61
  212.0 0.5 broadcast.59
  212.6 0.7 reduce.6
  213.6 35.1 %all-to-all-done.1 = bf16[48,2,8192]{2,1,0:T(2,128)(2,1)} async-done(((bf16[48,2,8192]{2,1,0:T(2,128)(2,1)}), bf16[48,2,8192]{2,1,0:T(2,128)(2,1)}, u32[]{:S(2)}, u32[]{:S(2)}) %all-to-all-start.1) | async-done | bytes 1572896 | tf_op jit(solution)/shard_map/all_to_all | solution.py:61
  248.7 8.1 %reshape.116 = bf16[48,1,16384]{2,1,0:T(2,128)(2,1)} reshape(bf16[48,2,8192]{2,1,0:T(2,128)(2,1)} %all-to-all-done.1) | data formatting | bytes 3145728
  256.9 12.4 %reduce.2 = bf16[48,16384]{1,0:T(8,128)(2,1)} reduce(bf16[48,1,16384]{2,1,0:T(2,128)(2,1)} %reshape.116, bf16[]{:T(256)} %constant.43), dimensions={1}, to_apply=%all_to_all.15.reduce_sub_computation | reduce | bytes 3145730 | tf_op jit(solution)/shard_map/all_to_all | solution.py:61
  269.3 3.8 %reshape.90 = bf16[1536,512]{1,0:T(8,128)(2,1)} reshape(bf16[48,16384]{1,0:T(8,128)(2,1)} %reduce.2) | data formatting | bytes 3145728 | tf_op jit(solution)/shard_map/reshape | solution.py:64
  273.1 10.7 %scatter_fusion = bf16[1536,512]{1,0:T(8,128)(2,1)} fusion(bf16[1536,512]{1,0:T(8,128)(2,1)} %copy.21, s32[1536]{0:T(1024)S(1)} %fusion.8, bf16[1536,512]{1,0:T(8,128)(2,1)} %reshape.90), kind=kCustom, calls=%fused_computation | custom fusion | bytes 4724736 | tf_op jit(solution)/shard_map/scatter | solution.py:72
  283.8 1.8 fusion
  285.6 48.6 %psum.7 = f32[1536]{0:T(1024)S(1)} all-reduce(f32[1536]{0:T(1024)S(1)} %fusion), channel_id=1, replica_groups=mesh['grp'=48,'dp'=16] {'dp'}, use_global_device_ids=true, to_apply=%region_5.6 | all-reduce | flops 1536 | bytes 12288 | tf_op jit(solution)/shard_map/psum | solution.py:74
  334.2 3.0 fusion.2
  (33 shorter events, 1.7 us)
Async XLA Ops:
  6.5 143.9 %copy-start = (bf16[3200,512]{1,0:T(8,128)(2,1)S(1)}, bf16[3200,512]{1,0:T(8,128)(2,1)}, u32[]{:S(2)}) copy-start(bf16[3200,512]{1,0:T(8,128)(2,1)} %param.11) | copy-start | bytes 9830404
  6.5 3.1 copy-start.2
  6.5 143.9 %copy-start.5 = (f32[512]{0:T(512)S(1)}, f32[512]{0:T(512)}, u32[]{:S(2)}) copy-start(f32[512]{0:T(512)} %param.12) | copy-start | bytes 6148
  6.5 6.6 %copy-start.6 = (s32[4]{0:T(128)S(1)}, s32[4]{0:T(128)}, u32[]{:S(2)}) copy-start(s32[4]{0:T(128)} %param.16) | copy-start | bytes 52
  6.5 6.9 %copy-start.4 = (s32[4]{0:T(128)S(1)}, s32[4]{0:T(128)}, u32[]{:S(2)}) copy-start(s32[4]{0:T(128)} %param.17) | copy-start | bytes 52
  6.5 143.9 %all-gather.2.cloned.1.call-start = ((), (), s32[]{:S(2)}) async-start(), calls=%async_computation.2 | async-start | bytes 6963200 | tf_op jit(solution)/shard_map/all_gather | solution.py:40
  6.6 2.8 copy-start.1
  43.9 145.3 %all-to-all-start = ((s32[48,1,2]{2,1,0:T(1,128)}), s32[48,1,2]{2,1,0:T(1,128)S(1)}, u32[]{:S(2)}, u32[]{:S(2)}) async-start(s32[48,1,2]{2,1,0:T(1,128)} %bitcast.2), calls=%async_computation | async-start | bytes 49152 | tf_op jit(solution)/shard_map/all_to_all | solution.py:62
  189.3 59.5 %all-to-all-start.1 = ((bf16[48,2,8192]{2,1,0:T(2,128)(2,1)}), bf16[48,2,8192]{2,1,0:T(2,128)(2,1)}, u32[]{:S(2)}, u32[]{:S(2)}) async-start(bf16[48,2,8192]{2,1,0:T(2,128)(2,1)} %reshape.115), calls=%async_computation.1 | async-start | bytes 3145728 | tf_op jit(solution)/shard_map/all_to_all | solution.py:61
  273.1 61.1 %copy-start.3 = (f32[512]{0:T(512)S(1)}, f32[512]{0:T(512)}, u32[]{:S(2)}) copy-start(f32[512]{0:T(512)} %param.14) | copy-start | bytes 6148
Sparse Core Ops, SparseCore 0:
  10.9 139.4 all-gather.1
where the time goes:
time: 345 us; the launch traced here: 344 us
  waiting for transfers between devices  133 us (39%)
  blocking collectives  78 us (23%)
  local copies, waits for them, and re-layouts  43.7 us (13%)
  other arithmetic  32.4 us (9%)
  starting transfers between devices  31.2 us (9%)
  between operations  14.8 us (4%)
  matrix products  10.6 us (3%)
    all_gather x1, waiting for transfers between devices, on_device(): lax.all_gather(normed, 'dp', axis=0, tiled=True)  98.1 us
    psum x1, blocking collectives, on_device(): row_total = lax.psum(local_squares, 'dp')  48.6 us
    all_to_all x1, waiting for transfers between devices, on_device(): lax.all_to_all(bucketed, 'grp', split_axis=0, concat_axis=0, tiled=True)  35.1 us
    unnamed x1, blocking collectives  29.4 us
    all_to_all x2, other arithmetic, on_device(): lax.all_to_all(bucketed, 'grp', split_axis=0, concat_axis=0, tiled=True)  25.4 us
    all_to_all x1, starting transfers between devices, on_device(): lax.all_to_all(bucketed, 'grp', split_axis=0, concat_axis=0, tiled=True)  22.8 us
    unnamed x21, local copies, waits for them, and re-layouts  16.4 us
    scatter x1, local copies, waits for them, and re-layouts, on_device(): merged = text_embed.at[target].set(received, mode='drop')  10.7 us
  transfers between devices with their start and end apart: 3, of which 2 were waited for; matrix products, arithmetic and copies ran while one was open for 10% of the time, Pallas kernels for 0%

commit v1 on v0

v1 whole, which is shorter than its diff:
```python
import functools

import jax
import jax.numpy as jnp
from jax import lax
from jax.experimental import pallas as pl
from jax.experimental.pallas import tpu as pltpu
from jax.sharding import PartitionSpec as P

MESH = pl.DeviceIdType.MESH
PATCH = 16
CAP = 2
DP_X = 4
DP_Z = 4
PIECES = 4
LANES = 128


def row_sums(values):
    f = values.astype(jnp.float32)
    sq = f * f
    part = sq[:, :LANES]
    for c in range(1, values.shape[1] // LANES):
        part = part + sq[:, c * LANES : (c + 1) * LANES]
    return jnp.sum(part.T, axis=0, keepdims=True)


def spread(row, columns):
    square = jnp.broadcast_to(row, (LANES, LANES)).T
    return jnp.concatenate([square] * (columns // LANES), axis=1)


def exchange_kernel(
    dims,
    vis_ref,
    vgain_ref,
    w_hbm,
    bias_ref,
    text_hbm,
    ogain_ref,
    count_ref,
    owner_ref,
    offset_ref,
    arrived_ref,
    places_ref,
    thid_hbm,
    gather,
    w_ref,
    text_ref,
    thid_ref,
    proj,
    outbox,
    meta,
    table,
    table_s,
    tstat,
    pstat,
    local_sem,
    zs_sem,
    zr_sem,
    xs_sem,
    xr_sem,
    g_sem,
    ms_sem,
    mr_sem,
    ts_sem,
    tr_sem,
    ps_sem,
    pr_sem,
    os_sem,
    or_sem,
    as_sem,
    ar_sem,
):
    groups, ranks, features = dims
    grp = lax.axis_index("grp")
    dp = lax.axis_index("dp")
    zi, xi = dp // DP_X, dp % DP_X
    up, down, zop = (zi + 1) % DP_Z, (zi + 3) % DP_Z, (zi + 2) % DP_Z
    right, left, xop = (xi + 1) % DP_X, (xi + 3) % DP_X, (xi + 2) % DP_X
    planes = (zi, down, up, zop)

    def remote(src, dst, ssem, rsem, **where):
        return pltpu.make_async_remote_copy(
            src_ref=src, dst_ref=dst, send_sem=ssem, recv_sem=rsem, device_id=where, device_id_type=MESH
        )

    w_copy = pltpu.make_async_copy(w_hbm, w_ref, local_sem.at[0])
    text_copy = pltpu.make_async_copy(text_hbm, text_ref, local_sem.at[1])
    w_copy.start()
    text_copy.start()

    barrier = pltpu.get_barrier_semaphore()

    @pl.loop(1, ranks)
    def _(k):
        pl.semaphore_signal(barrier, inc=1, device_id={"dp": (dp + k) % ranks}, device_id_type=MESH)

    @pl.loop(1, groups)
    def _(k):
        pl.semaphore_signal(barrier, inc=1, device_id={"grp": (grp + k) % groups}, device_id_type=MESH)

    f = vis_ref[...].astype(jnp.float32)
    normed = (
        f * lax.rsqrt(jnp.mean(f * f, axis=-1, keepdims=True) + 1e-06) * vgain_ref[...]
    ).astype(jnp.bfloat16)
    gather[dp] = normed.reshape(gather.shape[1:])

    lane = lax.broadcasted_iota(jnp.int32, (8, LANES), 1)
    owners = jnp.zeros((8, LANES), jnp.int32)
    places = jnp.zeros((8, LANES), jnp.int32)
    slots = owner_ref.shape[0]
    for j in range(slots):
        mine = lane == dp * slots + j
        owners = jnp.where(mine, owner_ref[j], owners)
        live = jnp.full((8, LANES), count_ref[0], jnp.int32) > j
        places = jnp.where(mine & live, offset_ref[j] + 1, places)
    meta[dp, 0] = owners
    meta[dp, 1] = places

    pl.semaphore_wait(barrier, ranks - 1 + groups - 1)

    def z_copy(plane, s, target, sem):
        piece = gather.at[plane * DP_X + xi, s]
        return remote(piece, piece, sem, g_sem.at[plane * DP_X + xi, s], dp=target * DP_X + xi)

    def x_copy(plane, source, s, target, sem):
        piece = gather.at[plane * DP_X + source, s]
        return remote(piece, piece, sem, g_sem.at[plane * DP_X + source, s], dp=zi * DP_X + target)

    sends = []

    def go(copy):
        copy.start()
        sends.append(copy)

    def send_x(q, s):
        go(x_copy(planes[q], xi, s, right, xs_sem.at[q, 0, s]))
        go(x_copy(planes[q], xi, s, left, xs_sem.at[q, 1, s]))

    def arrived_x(q, source, s):
        x_copy(planes[q], source, s, right, xs_sem.at[q, 0, s]).wait_recv()

    def relay_x(q, s):
        if s % 2 == 0:
            arrived_x(q, left, s)
            go(x_copy(planes[q], left, s, right, xr_sem.at[q, s]))
        else:
            arrived_x(q, right, s)
            go(x_copy(planes[q], right, s, left, xr_sem.at[q, s]))

    def finish_x(q):
        for s in range(PIECES):
            arrived_x(q, right if s % 2 == 0 else left, s)
            arrived_x(q, xop, s)

    def arrived_z(q, s):
        z_copy(planes[q], s, up, zs_sem.at[0, s]).wait_recv()

    for s in range(PIECES):
        go(z_copy(zi, s, up, zs_sem.at[0, s]))
        go(z_copy(zi, s, down, zs_sem.at[1, s]))
        send_x(0, s)

    def to_ranks(buffer, ssem, rsem, act):
        @pl.loop(1, ranks)
        def _(k):
            peer = (dp + k) % ranks
            act(remote(buffer.at[dp], buffer.at[dp], ssem.at[peer], rsem.at[dp], dp=peer))

    def from_ranks(buffer, ssem, rsem):
        @pl.loop(1, ranks)
        def _(k):
            peer = (dp + k) % ranks
            remote(buffer.at[peer], buffer.at[peer], ssem.at[peer], rsem.at[peer], dp=peer).wait_recv()

    start = lambda copy: copy.start()
    wait_send = lambda copy: copy.wait_send()

    to_ranks(meta, ms_sem, mr_sem, start)

    text_copy.wait()
    text_blocks = text_ref.shape[0]

    @pl.loop(0, text_blocks)
    def _(b):
        tstat[dp, b] = row_sums(text_ref[b])

    to_ranks(tstat, ts_sem, tr_sem, start)

    for s in range(PIECES):
        relay_x(0, s)

    def project(q):
        plane = planes[q]
        rows = gather[pl.ds(plane * DP_X, DP_X)]
        rows = rows.reshape(DP_X * PIECES * PATCH, rows.shape[-1])
        out = jnp.dot(rows, w_ref[...], preferred_element_type=jnp.float32) + bias_ref[...]
        out = out.astype(jnp.bfloat16)
        images = DP_X * PIECES
        proj[pl.ds(plane * images, images)] = out.reshape(images, PATCH, out.shape[-1])
        for b in range(2):
            pstat[dp, plane * 2 + b] = row_sums(out[b * LANES : (b + 1) * LANES])

    def tables():
        from_ranks(meta, ms_sem, mr_sem)
        owners = meta[0, 0]
        places = meta[0, 1]
        for r in range(1, ranks):
            owners = owners + meta[r, 0]
            places = places + meta[r, 1]
        owner_row = owners[:1][None]
        place_row = places[:1][None]
        shape = (groups, 1, LANES)
        slot = lax.broadcasted_iota(jnp.int32, shape, 2)
        group = lax.broadcasted_iota(jnp.int32, shape, 0)
        named = (owner_row == group) & (slot < ranks * slots)
        first = jnp.min(jnp.where(named, slot, LANES), axis=2, keepdims=True)
        last = jnp.max(jnp.where(named, slot, -1), axis=2, keepdims=True)
        at_first = jnp.max(jnp.where(named & (slot == first), place_row, 0), axis=2, keepdims=True)
        at_last = jnp.max(
            jnp.where(named & (slot == last) & (slot != first), place_row, 0), axis=2, keepdims=True
        )
        first = jnp.minimum(first, ranks * slots - 1)
        last = jnp.maximum(last, 0)
        values = jnp.where(slot == 0, at_first - 1, at_last - 1)
        values = jnp.where(slot == 2, first, values)
        values = jnp.where(slot == 3, last, values)
        table[...] = values

    def table_copy(peer):
        return remote(table.at[peer], places_ref.at[grp], os_sem.at[peer], or_sem.at[grp], grp=peer)

    def out_copy(peer):
        return remote(outbox.at[peer], arrived_ref.at[grp], as_sem.at[peer], ar_sem.at[grp], grp=peer)

    def to_groups(make, act):
        @pl.loop(1, groups)
        def _(k):
            act(make((grp + k) % groups))

    def text_hidden():
        from_ranks(tstat, ts_sem, tr_sem)

        @pl.loop(0, text_blocks)
        def _(b):
            total = tstat[0, b]
            for r in range(1, ranks):
                total = total + tstat[r, b]
            inverse = lax.rsqrt(total / features + 1e-05)
            rows = text_ref[b].astype(jnp.float32)
            rows = rows * spread(inverse, rows.shape[1]) * ogain_ref[...]
            thid_ref[b] = rows.astype(jnp.bfloat16)

    thid_copy = pltpu.make_async_copy(thid_ref, thid_hbm, local_sem.at[2])
    table_smem = pltpu.make_async_copy(table, table_s, local_sem.at[3])
    place_own = pltpu.make_async_copy(table.at[grp], places_ref.at[grp], local_sem.at[4])
    out_own = pltpu.make_async_copy(outbox.at[grp], arrived_ref.at[grp], local_sem.at[5])

    w_copy.wait()
    for s in range(PIECES):
        arrived_z(1, s)
        if s % 2 == 0:
            go(z_copy(down, s, up, zr_sem.at[s]))
        send_x(1, s)
        arrived_z(2, s)
        if s % 2 == 1:
            go(z_copy(up, s, down, zr_sem.at[s]))
        send_x(2, s)
        if s >= 1:
            relay_x(1, s - 1)
            relay_x(2, s - 1)
        if s == 0:
            tables()
            table_smem.start()
            place_own.start()
            to_groups(table_copy, start)
        if s == 1:
            finish_x(0)
            project(0)
        if s == 2:
            text_hidden()
            thid_copy.start()

    for s in range(PIECES):
        arrived_z(3, s)
        send_x(3, s)
        if s == 1:
            relay_x(1, PIECES - 1)
            relay_x(2, PIECES - 1)
            relay_x(3, 0)
        if s == 2:
            finish_x(1)
            project(1)
            relay_x(3, 1)
    finish_x(2)
    project(2)
    relay_x(3, 2)
    relay_x(3, 3)
    finish_x(3)
    project(3)

    to_ranks(pstat, ps_sem, pr_sem, start)
    table_smem.wait()
    from_ranks(pstat, ps_sem, pr_sem)

    @pl.loop(0, pstat.shape[1])
    def _(b):
        total = pstat[0, b]
        for r in range(1, ranks):
            total = total + pstat[r, b]
        inverse = lax.rsqrt(total / features + 1e-05)
        images = LANES // PATCH
        rows = proj[pl.ds(b * images, images)]
        shape = rows.shape
        rows = rows.reshape(LANES, shape[-1]).astype(jnp.float32)
        rows = rows * spread(inverse, shape[-1]) * ogain_ref[...]
        proj[pl.ds(b * images, images)] = rows.astype(jnp.bfloat16).reshape(shape)

    @pl.loop(0, groups)
    def _(o):
        for r in range(CAP):
            outbox[o, r] = proj[table_s[o, 0, CAP + r]]

    to_groups(out_copy, start)
    out_own.start()

    to_ranks(meta, ms_sem, mr_sem, wait_send)
    to_ranks(tstat, ts_sem, tr_sem, wait_send)
    to_ranks(pstat, ps_sem, pr_sem, wait_send)
    to_groups(table_copy, wait_send)
    for copy in sends:
        copy.wait_send()
    thid_copy.wait()
    place_own.wait()

    @pl.loop(1, groups)
    def _(k):
        peer = (grp + k) % groups
        remote(table.at[peer], places_ref.at[peer], os_sem.at[peer], or_sem.at[peer], grp=peer).wait_recv()

    @pl.loop(1, groups)
    def _(k):
        peer = (grp + k) % groups
        remote(outbox.at[peer], arrived_ref.at[peer], as_sem.at[peer], ar_sem.at[peer], grp=peer).wait()

    out_own.wait()


def overlay_kernel(places_ref, thid_ref, arrived_ref, out_ref, rows):
    chunks = rows.shape[0]
    for c in range(chunks):
        rows[c] = thid_ref[:, c * LANES : (c + 1) * LANES].astype(jnp.float32)

    @pl.loop(0, arrived_ref.shape[0])
    def _(g):
        for r in range(CAP):
            at = places_ref[g, 0, r]

            @pl.when(at >= 0)
            def _():
                image = arrived_ref[g, r].astype(jnp.float32)
                for c in range(chunks):
                    rows[c, pl.ds(at, PATCH), :] = image[:, c * LANES : (c + 1) * LANES]

    for c in range(chunks):
        out_ref[:, c * LANES : (c + 1) * LANES] = rows[c].astype(jnp.bfloat16)


def on_device(
    ranks,
    vis_features,
    vis_gain,
    proj_weight,
    proj_bias,
    text_embed,
    out_gain,
    image_counts,
    owner_block,
    offsets,
):
    groups = lax.axis_size("grp")
    width, columns = proj_weight.shape
    seq_len = text_embed.shape[0]
    slots = ranks * owner_block.shape[0]
    text_blocks = seq_len // LANES
    stat_blocks = slots * PATCH // LANES
    bf16, f32, i32 = jnp.bfloat16, jnp.float32, jnp.int32
    vmem = pl.BlockSpec(memory_space=pltpu.VMEM)
    smem = pl.BlockSpec(memory_space=pltpu.SMEM)
    hbm = pl.BlockSpec(memory_space=pl.ANY)
    dma = pltpu.SemaphoreType.DMA
    arrived, places, thid = pl.pallas_call(
        functools.partial(exchange_kernel, (groups, ranks, ranks * columns)),
        out_shape=(
            jax.ShapeDtypeStruct((groups, CAP, PATCH, columns), bf16),
            jax.ShapeDtypeStruct((groups, 1, LANES), i32),
            jax.ShapeDtypeStruct((text_blocks, LANES, columns), bf16),
        ),
        in_specs=[vmem, vmem, hbm, vmem, hbm, vmem, smem, smem, smem],
        out_specs=(hbm, hbm, hbm),
        scratch_shapes=[
            pltpu.VMEM((ranks, PIECES, PATCH, width), bf16),
            pltpu.VMEM((width, columns), bf16),
            pltpu.VMEM((text_blocks, LANES, columns), bf16),
            pltpu.VMEM((text_blocks, LANES, columns), bf16),
            pltpu.VMEM((slots, PATCH, columns), bf16),
            pltpu.VMEM((groups, CAP, PATCH, columns), bf16),
            pltpu.VMEM((ranks, 2, 8, LANES), i32),
            pltpu.VMEM((groups, 1, LANES), i32),
            pltpu.SMEM((groups, 1, LANES), i32),
            pltpu.VMEM((ranks, text_blocks, 1, LANES), f32),
            pltpu.VMEM((ranks, stat_blocks, 1, LANES), f32),
            dma((6,)),
            dma((2, PIECES)),
            dma((PIECES,)),
            dma((DP_Z, 2, PIECES)),
            dma((DP_Z, PIECES)),
            dma((ranks, PIECES)),
            dma((ranks,)),
            dma((ranks,)),
            dma((ranks,)),
            dma((ranks,)),
            dma((ranks,)),
            dma((ranks,)),
            dma((groups,)),
            dma((groups,)),
            dma((groups,)),
            dma((groups,)),
        ],
        compiler_params=pltpu.CompilerParams(
            collective_id=0, has_side_effects=True, vmem_limit_bytes=48 << 20
        ),
        name="exchange",
    )(
        vis_features,
        vis_gain.reshape(1, width),
        proj_weight,
        proj_bias.reshape(1, columns),
        text_embed.reshape(text_blocks, LANES, columns),
        out_gain.reshape(1, columns),
        image_counts,
        owner_block,
        offsets,
    )
    return pl.pallas_call(
        overlay_kernel,
        out_shape=jax.ShapeDtypeStruct((seq_len, columns), bf16),
        in_specs=[smem, vmem, vmem],
        out_specs=vmem,
        scratch_shapes=[pltpu.VMEM((columns // LANES, seq_len, LANES), f32)],
        compiler_params=pltpu.CompilerParams(vmem_limit_bytes=32 << 20),
        name="overlay",
    )(places, thid.reshape(seq_len, columns), arrived)


def solution(mesh):
    return jax.shard_map(
        functools.partial(on_device, mesh.shape["dp"]),
        mesh=mesh,
        in_specs=(
            P(("grp", "dp"), None),
            P(),
            P(None, "dp"),
            P("dp"),
            P("grp", "dp"),
            P("dp"),
            P(("grp", "dp")),
            P(("grp", "dp")),
            P(("grp", "dp")),
        ),
        out_specs=P("grp", "dp"),
        check_vma=False,
    )
```

time: 345 us -> 163 us (0.47)
  the two profiles are of different devices: /device:TPU:8 before, /device:TPU:69 now
where the time goes in v1:
time: 163 us
  Pallas kernels  156 us (96%)
  local copies, waits for them, and re-layouts  5.8 us (4%)
    pallas_call x1, Pallas kernels, on_device(): pl.pallas_call(functools.partial(exchange_kernel, (groups, ranks, ranks *...  152 us
    unnamed x12, local copies, waits for them, and re-layouts  5.08 us
    pallas_call x1, Pallas kernels, on_device(): pl.pallas_call(overlay_kernel, out_shape=jax.ShapeDtypeStruct((seq_len, c...  3.68 us

profile of v1, /device:TPU:69, one launch (start us, length us, event | category | flops | bytes accessed | tf_op | source)
XLA Modules:
  0.0 162.5 jit_solution(17025269039748238540)
XLA Ops:
  0.7 0.7 reshape.15.vgain_ref
  1.4 0.0 copy-start
  1.4 1.4 copy-done
  2.8 0.0 copy-start.1
  2.8 1.0 copy-done.1
  3.8 0.0 copy-start.2
  3.8 0.7 copy-done.2
  4.5 0.0 copy-start.3
  4.5 0.7 copy-done.3
  5.2 0.0 copy-start.4
  5.2 0.7 copy-done.4
  5.8 0.0 copy-start.5
  5.8 0.7 copy-done.5
  6.5 152.3 %exchange.1 = (bf16[48,2,16,512]{3,2,1,0:T(8,128)(2,1)S(1)}, s32[48,1,128]{2,1,0:T(1,128)S(1)}, bf16[12,128,512]{2,1,0:T(8,128)(2,1)S(1)}) custom-call(bf16[64,3200]{1,0:T(8,128)(2,1)S(1)} %copy-done.1, f32[1,3200]{1,0:T(1,128)S(1)} %reshape.15.vgain_ref, bf16[3200,512]{1,0:T(8,128)(2,1)} %w_hbm.1, f32[1,512]{1,0:T(1,128)S(1)} %bitcast.6, ...), custom_call_target="tpu_custom_call" | custom-call | tf_op jit(solution)/shard_map/exchange/pallas_call | solution.py:393
  158.8 3.7 %overlay.1 = bf16[1536,512]{1,0:T(8,128)(2,1)} custom-call(s32[48,1,128]{2,1,0:T(1,128)S(1)} %get-tuple-element.8.places_ref, bf16[1536,512]{1,0:T(8,128)(2,1)S(1)} %bitcast.5, bf16[48,2,16,512]{3,2,1,0:T(8,128)(2,1)S(1)} %get-tuple-element.10.arrived_ref), custom_call_target="tpu_custom_call" | custom-call | tf_op jit(solution)/shard_map/overlay/pallas_call | solution.py:446
Async XLA Ops:
  1.4 1.4 copy-start
  2.8 1.0 copy-start.1
  3.8 0.7 copy-start.2
  4.5 0.7 copy-start.3
  5.2 0.7 copy-start.4
  5.8 0.7 copy-start.5

commit v2 on v1

v2 whole, which is shorter than its diff:
```python
import functools

import jax
import jax.numpy as jnp
from jax import lax
from jax.experimental import pallas as pl
from jax.experimental.pallas import tpu as pltpu
from jax.sharding import PartitionSpec as P

MESH = pl.DeviceIdType.MESH
PATCH = 16
CAP = 2
DP_X = 4
DP_Z = 4
PIECES = 4
Z_LO = 3
CORES = 2
SPAN = 2048
LANES = 128


def row_sums(values):
    f = values.astype(jnp.float32)
    sq = f * f
    part = sq[:, :LANES]
    for c in range(1, values.shape[1] // LANES):
        part = part + sq[:, c * LANES : (c + 1) * LANES]
    return jnp.sum(part.T, axis=0, keepdims=True)


def spread(row, columns):
    square = jnp.broadcast_to(row, (LANES, LANES)).T
    return jnp.concatenate([square] * (columns // LANES), axis=1)


def arrival_order(piece=2.2, latency=1.6, ahead=3):
    free = dict.fromkeys("UDRL", 0.0)
    now = 0.0
    pending = {}
    order = []

    def send(link, key):
        free[link] = max(free[link], now) + piece
        pending[key] = free[link] + latency

    def own(s):
        order.append(("own", s))
        for d in "UD":
            send(d, ("z", d, 1, s))

    def across(q, s):
        for d in "RL":
            send(d, ("x", q, d, 1, s))

    for s in range(PIECES):
        if s < ahead:
            own(s)
        order.append(("ownx", s))
        across(0, s)
    following = ahead
    count = [0] * DP_Z
    tasks = [(0.0, "tstat", 2.0), (8.0, "tables", 1.5), (9.0, "text2", 0.3), (20.0, "text3", 2.5)]
    while pending or tasks:
        here = [k for k, t in pending.items() if t <= now]
        ready = [t for t in tasks if t[0] <= now]
        if not here and ready:
            tasks.remove(ready[0])
            order.append(("task", ready[0][1]))
            now += ready[0][2]
            continue
        if not here:
            now = min([*pending.values(), *[t[0] for t in tasks]])
            continue
        key = min(here, key=lambda k: pending[k])
        del pending[key]
        order.append(key)
        now += 0.06
        if key[0] == "z":
            _, d, age, s = key
            if goes_on(d, age, s):
                send(d, ("z", d, age + 1, s))
            if age % Z_LO == 0:
                across(plane_of(d, age), s)
            if age == 1 and d == "D" and following < PIECES:
                own(following)
                following += 1
        else:
            _, q, d, age, s = key
            if age == 1 and s % 2 == (d == "L"):
                send(d, ("x", q, d, 2, s))
            count[q] += 1
            if count[q] == (DP_X - 1) * PIECES:
                tasks.append((now, q, 3.0))
    return order


def goes_on(d, age, s):
    return age < Z_LO or (age < 2 * Z_LO and s % 2 == (d == "D"))


def plane_of(d, age):
    return 3 if age == 2 * Z_LO else 1 if d == "U" else 2


def exchange_kernel(
    dims,
    vis_hbm,
    vgain_hbm,
    w_hbm,
    bias_hbm,
    text_hbm,
    ogain_hbm,
    count_hbm,
    owner_hbm,
    offset_hbm,
    arrived_ref,
    places_ref,
    thid_hbm,
    vis_ref,
    vgain_ref,
    bias_ref,
    ogain_ref,
    count_ref,
    owner_ref,
    offset_ref,
    gather,
    passing,
    w_ref,
    text_ref,
    thid_ref,
    proj,
    outbox,
    meta,
    table,
    table_s,
    tstat_x,
    tstat_z,
    pstat_x,
    pstat_z,
    local_sem,
    zs_sem,
    zg_sem,
    xs_sem,
    xr_sem,
    g_sem,
    ms_sem,
    mr_sem,
    ts_sem,
    tr_sem,
    ps_sem,
    pr_sem,
    os_sem,
    or_sem,
    as_sem,
    ar_sem,
):
    groups, ranks, features = dims
    grp = lax.axis_index("grp")
    dp = lax.axis_index("dp")
    zi, xi = dp // DP_X, dp % DP_X
    core, z_lo, y = grp % CORES, grp // CORES % Z_LO, grp // CORES // Z_LO
    z = zi * Z_LO + z_lo
    z_ring = DP_Z * Z_LO
    planes = (zi, (zi + 3) % DP_Z, (zi + 1) % DP_Z, (zi + 2) % DP_Z)
    x_next = {"R": (xi + 1) % DP_X, "L": (xi + 3) % DP_X}
    x_from = {"R": (xi + 3) % DP_X, "L": (xi + 1) % DP_X}
    x_far = (xi + 2) % DP_X

    def z_device(at):
        return {"grp": (y * Z_LO + at % Z_LO) * CORES + core, "dp": at // Z_LO * DP_X + xi}

    z_next = {"U": z_device((z + 1) % z_ring), "D": z_device((z + z_ring - 1) % z_ring)}

    def remote(src, dst, ssem, rsem, **where):
        return pltpu.make_async_remote_copy(
            src_ref=src, dst_ref=dst, send_sem=ssem, recv_sem=rsem, device_id=where, device_id_type=MESH
        )

    loads = [
        pltpu.make_async_copy(src, dst, local_sem.at[4 + n])
        for n, (src, dst) in enumerate(
            [
                (vis_hbm, vis_ref),
                (vgain_hbm, vgain_ref),
                (owner_hbm, owner_ref),
                (offset_hbm, offset_ref),
                (count_hbm, count_ref),
                (bias_hbm, bias_ref),
                (ogain_hbm, ogain_ref),
                (text_hbm, text_ref),
                (w_hbm, w_ref),
            ]
        )
    ]
    for copy in loads:
        copy.start()

    barrier = pltpu.get_barrier_semaphore()

    for d in "UD":
        pl.semaphore_signal(barrier, inc=1, device_id=z_next[d], device_id_type=MESH)

    @pl.loop(1, ranks)
    def _(k):
        pl.semaphore_signal(barrier, inc=1, device_id={"dp": (dp + k) % ranks}, device_id_type=MESH)

    @pl.loop(1, groups)
    def _(k):
        pl.semaphore_signal(barrier, inc=1, device_id={"grp": (grp + k) % groups}, device_id_type=MESH)

    for copy in loads[:7]:
        copy.wait()
    f = vis_ref[...].astype(jnp.float32)
    normed = (
        f * lax.rsqrt(jnp.mean(f * f, axis=-1, keepdims=True) + 1e-06) * vgain_ref[...]
    ).astype(jnp.bfloat16)
    gather[dp] = normed.reshape(gather.shape[1:])

    lane = lax.broadcasted_iota(jnp.int32, (1, LANES), 1)
    packed = jnp.zeros((1, LANES), jnp.int32)
    slots = owner_ref.shape[0]
    for j in range(slots):
        live = jnp.full((1, LANES), count_ref[0], jnp.int32) > j
        value = owner_ref[j] * SPAN + jnp.where(live, offset_ref[j] + 1, 0)
        packed = jnp.where(lane == dp * slots + j, value, packed)
    meta[dp] = packed

    pl.semaphore_wait(barrier, ranks - 1 + groups - 1 + 2)

    def z_source(d, age):
        return ((z + z_ring - age if d == "U" else z + age) % z_ring) // Z_LO

    def z_slot(d, age, s, arriving):
        if age % Z_LO == 0:
            return gather.at[z_source(d, age) * DP_X + xi, s]
        return passing.at["UD".index(d), age - 1 - age // Z_LO, s]

    def z_copy(d, age, s):
        if age % Z_LO == 0:
            target = gather.at[z_source(d, age - 1) * DP_X + xi, s]
        else:
            target = passing.at["UD".index(d), age - 1 - age // Z_LO, s]
        n = "UD".index(d)
        return remote(
            z_slot(d, age - 1, s, False), target, zs_sem.at[n, age - 1, s], zg_sem.at[n, age - 1, s], **z_next[d]
        )

    def z_arrival(d, age, s):
        n = "UD".index(d)
        piece = z_slot(d, age, s, True)
        return remote(piece, piece, zs_sem.at[n, age - 1, s], zg_sem.at[n, age - 1, s], **z_next[d])

    def x_copy(q, source, d, s, sem):
        place = planes[q] * DP_X + source
        piece = gather.at[place, s]
        return remote(piece, piece, sem, g_sem.at[place, s], dp=zi * DP_X + x_next[d])

    sends = []

    def go(copy):
        copy.start()
        sends.append(copy)

    def across(q, s):
        for n, d in enumerate("RL"):
            go(x_copy(q, xi, d, s, xs_sem.at[q, n, s]))

    def to_ranks(act):
        @pl.loop(1, ranks)
        def _(k):
            peer = (dp + k) % ranks
            act(remote(meta.at[dp], meta.at[dp], ms_sem.at[peer], mr_sem.at[dp], dp=peer))

    start = lambda copy: copy.start()
    wait_send = lambda copy: copy.wait_send()

    def x_stats(buffer, ssem, rsem, k, mine):
        peer = (xi + k) % DP_X
        slot = xi if mine else peer
        return remote(buffer.at[slot], buffer.at[slot], ssem.at[peer], rsem.at[slot], dp=zi * DP_X + peer)

    def z_stats(buffer, ssem, rsem, k, mine):
        peer = (zi + k) % DP_Z
        slot = zi if mine else peer
        return remote(
            buffer.at[slot],
            buffer.at[slot],
            ssem.at[DP_X + peer],
            rsem.at[DP_X + slot],
            dp=peer * DP_X + xi,
        )

    def stats_start(stage, buffer, ssem, rsem):
        for k in range(1, 4):
            go(stage(buffer, ssem, rsem, k, True))

    def stats_sum(stage, buffer, ssem, rsem):
        for k in range(1, 4):
            stage(buffer, ssem, rsem, k, False).wait_recv()
        return (buffer[0] + buffer[1]) + (buffer[2] + buffer[3])

    text_blocks = text_ref.shape[0]

    def project(q):
        plane = planes[q]
        rows = gather[pl.ds(plane * DP_X, DP_X)]
        rows = rows.reshape(DP_X * PIECES * PATCH, rows.shape[-1])
        out = jnp.dot(rows, w_ref[...], preferred_element_type=jnp.float32) + bias_ref[...]
        out = out.astype(jnp.bfloat16)
        images = DP_X * PIECES
        proj[pl.ds(plane * images, images)] = out.reshape(images, PATCH, out.shape[-1])
        for b in range(2):
            pstat_x[xi, plane * 2 + b] = row_sums(out[b * LANES : (b + 1) * LANES])

    def tables():
        @pl.loop(1, ranks)
        def _(k):
            peer = (dp + k) % ranks
            remote(meta.at[peer], meta.at[peer], ms_sem.at[peer], mr_sem.at[peer], dp=peer).wait_recv()

        packed = meta[0]
        for r in range(1, ranks):
            packed = packed + meta[r]
        packed = packed[None]
        owner_row = packed // SPAN
        place_row = packed % SPAN
        shape = (groups, 1, LANES)
        slot = lax.broadcasted_iota(jnp.int32, shape, 2)
        group = lax.broadcasted_iota(jnp.int32, shape, 0)
        named = (owner_row == group) & (slot < ranks * slots)
        first = jnp.min(jnp.where(named, slot, LANES), axis=2, keepdims=True)
        last = jnp.max(jnp.where(named, slot, -1), axis=2, keepdims=True)
        at_first = jnp.max(jnp.where(named & (slot == first), place_row, 0), axis=2, keepdims=True)
        at_last = jnp.max(
            jnp.where(named & (slot == last) & (slot != first), place_row, 0), axis=2, keepdims=True
        )
        first = jnp.minimum(first, ranks * slots - 1)
        last = jnp.maximum(last, 0)
        values = jnp.where(slot == 0, at_first - 1, at_last - 1)
        values = jnp.where(slot == 2, first, values)
        values = jnp.where(slot == 3, last, values)
        table[...] = values
        table_smem.start()
        place_own.start()
        to_groups(table_copy, start)

    def table_copy(peer):
        return remote(table.at[peer], places_ref.at[grp], os_sem.at[peer], or_sem.at[grp], grp=peer)

    def out_copy(peer):
        return remote(outbox.at[peer], arrived_ref.at[grp], as_sem.at[peer], ar_sem.at[grp], grp=peer)

    def to_groups(make, act):
        @pl.loop(1, groups)
        def _(k):
            act(make((grp + k) % groups))

    def text_first():
        loads[7].wait()

        @pl.loop(0, text_blocks)
        def _(b):
            tstat_x[xi, b] = row_sums(text_ref[b])

        stats_start(x_stats, tstat_x, ts_sem, tr_sem)

    def text_second():
        tstat_z[zi] = stats_sum(x_stats, tstat_x, ts_sem, tr_sem)
        stats_start(z_stats, tstat_z, ts_sem, tr_sem)

    def text_third():
        for k in range(1, 4):
            z_stats(tstat_z, ts_sem, tr_sem, k, False).wait_recv()

        @pl.loop(0, text_blocks)
        def _(b):
            total = (tstat_z[0, b] + tstat_z[1, b]) + (tstat_z[2, b] + tstat_z[3, b])
            inverse = lax.rsqrt(total / features + 1e-05)
            rows = text_ref[b].astype(jnp.float32)
            rows = rows * spread(inverse, rows.shape[1]) * ogain_ref[...]
            thid_ref[b] = rows.astype(jnp.bfloat16)

        thid_copy.start()

    thid_copy = pltpu.make_async_copy(thid_ref, thid_hbm, local_sem.at[0])
    table_smem = pltpu.make_async_copy(table, table_s, local_sem.at[1])
    place_own = pltpu.make_async_copy(table.at[grp], places_ref.at[grp], local_sem.at[2])
    out_own = pltpu.make_async_copy(outbox.at[grp], arrived_ref.at[grp], local_sem.at[3])
    work = {"tstat": text_first, "tables": tables, "text2": text_second, "text3": text_third}

    opened = False
    for step in arrival_order():
        if step[0] == "own":
            for d in "UD":
                go(z_copy(d, 1, step[1]))
        elif step[0] == "ownx":
            across(0, step[1])
            if step[1] == PIECES - 1:
                to_ranks(start)
        elif step[0] == "task":
            if step[1] in work:
                work[step[1]]()
            else:
                if not opened:
                    loads[8].wait()
                    opened = True
                project(step[1])
        elif step[0] == "z":
            _, d, age, s = step
            z_arrival(d, age, s).wait_recv()
            if goes_on(d, age, s):
                go(z_copy(d, age + 1, s))
            if age % Z_LO == 0:
                across(plane_of(d, age), s)
        else:
            _, q, d, age, s = step
            source = x_from[d] if age == 1 else x_far
            x_copy(q, source, d, s, xr_sem.at[q, s]).wait_recv()
            if age == 1 and s % 2 == (d == "L"):
                go(x_copy(q, source, d, s, xr_sem.at[q, s]))

    stats_start(x_stats, pstat_x, ps_sem, pr_sem)
    table_smem.wait()
    pstat_z[zi] = stats_sum(x_stats, pstat_x, ps_sem, pr_sem)
    stats_start(z_stats, pstat_z, ps_sem, pr_sem)
    for k in range(1, 4):
        z_stats(pstat_z, ps_sem, pr_sem, k, False).wait_recv()

    @pl.loop(0, pstat_z.shape[1])
    def _(b):
        total = (pstat_z[0, b] + pstat_z[1, b]) + (pstat_z[2, b] + pstat_z[3, b])
        inverse = lax.rsqrt(total / features + 1e-05)
        images = LANES // PATCH
        rows = proj[pl.ds(b * images, images)]
        shape = rows.shape
        rows = rows.reshape(LANES, shape[-1]).astype(jnp.float32)
        rows = rows * spread(inverse, shape[-1]) * ogain_ref[...]
        proj[pl.ds(b * images, images)] = rows.astype(jnp.bfloat16).reshape(shape)

    @pl.loop(0, groups)
    def _(o):
        for r in range(CAP):
            outbox[o, r] = proj[table_s[o, 0, CAP + r]]

    to_groups(out_copy, start)
    out_own.start()

    to_ranks(wait_send)
    to_groups(table_copy, wait_send)
    for copy in sends:
        copy.wait_send()
    thid_copy.wait()
    place_own.wait()

    @pl.loop(1, groups)
    def _(k):
        peer = (grp + k) % groups
        remote(table.at[peer], places_ref.at[peer], os_sem.at[peer], or_sem.at[peer], grp=peer).wait_recv()

    @pl.loop(1, groups)
    def _(k):
        peer = (grp + k) % groups
        remote(outbox.at[peer], arrived_ref.at[peer], as_sem.at[peer], ar_sem.at[peer], grp=peer).wait()

    out_own.wait()


def overlay_kernel(places_ref, thid_ref, arrived_ref, out_ref, rows):
    chunks = rows.shape[0]
    for c in range(chunks):
        rows[c] = thid_ref[:, c * LANES : (c + 1) * LANES].astype(jnp.float32)

    @pl.loop(0, arrived_ref.shape[0])
    def _(g):
        for r in range(CAP):
            at = places_ref[g, 0, r]

            @pl.when(at >= 0)
            def _():
                image = arrived_ref[g, r].astype(jnp.float32)
                for c in range(chunks):
                    rows[c, pl.ds(at, PATCH), :] = image[:, c * LANES : (c + 1) * LANES]

    for c in range(chunks):
        out_ref[:, c * LANES : (c + 1) * LANES] = rows[c].astype(jnp.bfloat16)


def on_device(
    ranks,
    vis_features,
    vis_gain,
    proj_weight,
    proj_bias,
    text_embed,
    out_gain,
    image_counts,
    owner_block,
    offsets,
):
    groups = lax.axis_size("grp")
    width, columns = proj_weight.shape
    seq_len = text_embed.shape[0]
    slots = ranks * owner_block.shape[0]
    text_blocks = seq_len // LANES
    stat_blocks = slots * PATCH // LANES
    bf16, f32, i32 = jnp.bfloat16, jnp.float32, jnp.int32
    vmem = pl.BlockSpec(memory_space=pltpu.VMEM)
    smem = pl.BlockSpec(memory_space=pltpu.SMEM)
    hbm = pl.BlockSpec(memory_space=pltpu.HBM)
    dma = pltpu.SemaphoreType.DMA
    arrived, places, thid = pl.pallas_call(
        functools.partial(exchange_kernel, (groups, ranks, ranks * columns)),
        out_shape=(
            jax.ShapeDtypeStruct((groups, CAP, PATCH, columns), bf16),
            jax.ShapeDtypeStruct((groups, 1, LANES), i32),
            jax.ShapeDtypeStruct((text_blocks, LANES, columns), bf16),
        ),
        in_specs=[hbm] * 9,
        out_specs=(pl.BlockSpec(memory_space=pl.ANY),) * 3,
        scratch_shapes=[
            pltpu.VMEM(vis_features.shape, bf16),
            pltpu.VMEM((width,), f32),
            pltpu.VMEM((columns,), f32),
            pltpu.VMEM((columns,), f32),
            pltpu.SMEM(image_counts.shape, i32),
            pltpu.SMEM(owner_block.shape, i32),
            pltpu.SMEM(offsets.shape, i32),
            pltpu.VMEM((ranks, PIECES, PATCH, width), bf16),
            pltpu.VMEM((2, 2 * Z_LO - 2, PIECES, PATCH, width), bf16),
            pltpu.VMEM((width, columns), bf16),
            pltpu.VMEM((text_blocks, LANES, columns), bf16),
            pltpu.VMEM((text_blocks, LANES, columns), bf16),
            pltpu.VMEM((slots, PATCH, columns), bf16),
            pltpu.VMEM((groups, CAP, PATCH, columns), bf16),
            pltpu.VMEM((ranks, 1, LANES), i32),
            pltpu.VMEM((groups, 1, LANES), i32),
            pltpu.SMEM((groups, 1, LANES), i32),
            pltpu.VMEM((DP_X, text_blocks, 1, LANES), f32),
            pltpu.VMEM((DP_Z, text_blocks, 1, LANES), f32),
            pltpu.VMEM((DP_X, stat_blocks, 1, LANES), f32),
            pltpu.VMEM((DP_Z, stat_blocks, 1, LANES), f32),
            dma((13,)),
            dma((2, 2 * Z_LO, PIECES)),
            dma((2, 2 * Z_LO, PIECES)),
            dma((DP_Z, 2, PIECES)),
            dma((DP_Z, PIECES)),
            dma((ranks, PIECES)),
            dma((ranks,)),
            dma((ranks,)),
            dma((DP_X + DP_Z,)),
            dma((DP_X + DP_Z,)),
            dma((DP_X + DP_Z,)),
            dma((DP_X + DP_Z,)),
            dma((groups,)),
            dma((groups,)),
            dma((groups,)),
            dma((groups,)),
        ],
        compiler_params=pltpu.CompilerParams(
            collective_id=0, has_side_effects=True, vmem_limit_bytes=48 << 20
        ),
        name="exchange",
    )(
        vis_features,
        vis_gain,
        proj_weight,
        proj_bias,
        text_embed.reshape(text_blocks, LANES, columns),
        out_gain,
        image_counts,
        owner_block,
        offsets,
    )
    return pl.pallas_call(
        overlay_kernel,
        out_shape=jax.ShapeDtypeStruct((seq_len, columns), bf16),
        in_specs=[smem, vmem, vmem],
        out_specs=vmem,
        scratch_shapes=[pltpu.VMEM((columns // LANES, seq_len, LANES), f32)],
        compiler_params=pltpu.CompilerParams(vmem_limit_bytes=32 << 20),
        name="overlay",
    )(places, thid.reshape(seq_len, columns), arrived)


def solution(mesh):
    return jax.shard_map(
        functools.partial(on_device, mesh.shape["dp"]),
        mesh=mesh,
        in_specs=(
            P(("grp", "dp"), None),
            P(),
            P(None, "dp"),
            P("dp"),
            P("grp", "dp"),
            P("dp"),
            P(("grp", "dp")),
            P(("grp", "dp")),
            P(("grp", "dp")),
        ),
        out_specs=P("grp", "dp"),
        check_vma=False,
    )
```

time: 163 us -> 149 us (0.914)
  the two profiles are of different devices: /device:TPU:69 before, /device:TPU:279 now
where the time goes in v2:
time: 149 us
  Pallas kernels  142 us (95%)
  local copies, waits for them, and re-layouts  5.79 us (4%)
    pallas_call x1, Pallas kernels, on_device(): pl.pallas_call(functools.partial(exchange_kernel, (groups, ranks, ranks *...  139 us
    unnamed x14, local copies, waits for them, and re-layouts  5.79 us
    pallas_call x1, Pallas kernels, on_device(): pl.pallas_call(overlay_kernel, out_shape=jax.ShapeDtypeStruct((seq_len, c...  3.69 us

profile of v2, /device:TPU:279, one launch (start us, length us, event | category | flops | bytes accessed | tf_op | source)
XLA Modules:
  0.0 148.7 jit_solution(17618373706109256926)
XLA Ops:
  0.7 0.0 copy-start
  0.7 1.4 copy-done
  2.1 0.0 copy-start.1
  2.1 1.0 copy-done.1
  3.1 0.0 copy-start.2
  3.1 0.7 copy-done.2
  3.8 0.0 copy-start.3
  3.8 0.7 copy-done.3
  4.5 0.0 copy-start.4
  4.5 0.7 copy-done.4
  5.1 0.0 copy-start.5
  5.1 0.7 copy-done.5
  5.8 0.0 copy-start.6
  5.8 0.7 copy-done.6
  6.5 138.6 %exchange.1 = (bf16[48,2,16,512]{3,2,1,0:T(8,128)(2,1)S(1)}, s32[48,1,128]{2,1,0:T(1,128)S(1)}, bf16[12,128,512]{2,1,0:T(8,128)(2,1)S(1)}) custom-call(bf16[64,3200]{1,0:T(8,128)(2,1)S(1)} %copy-done.1, f32[3200]{0:T(1024)S(1)} %copy-done.2, bf16[3200,512]{1,0:T(8,128)(2,1)} %w_hbm.1, f32[512]{0:T(512)S(1)} %copy-done.3, bf16[12,128,512]{2,1,0:T(8,128)(2,1)S(1)} %bitcast.2, ...), custom_call_target="tpu_custom_call" | custom-call | tf_op jit(solution)/shard_map/exchange/pallas_call | solution.py:511
  145.1 3.7 %overlay.1 = bf16[1536,512]{1,0:T(8,128)(2,1)} custom-call(s32[48,1,128]{2,1,0:T(1,128)S(1)} %get-tuple-element.8.places_ref, bf16[1536,512]{1,0:T(8,128)(2,1)S(1)} %bitcast.3, bf16[48,2,16,512]{3,2,1,0:T(8,128)(2,1)S(1)} %get-tuple-element.10.arrived_ref), custom_call_target="tpu_custom_call" | custom-call | tf_op jit(solution)/shard_map/overlay/pallas_call | solution.py:574
Async XLA Ops:
  0.7 1.4 copy-start
  2.1 1.0 copy-start.1
  3.1 0.7 copy-start.2
  3.8 0.7 copy-start.3
  4.5 0.7 copy-start.4
  5.1 0.7 copy-start.5
  5.8 0.7 copy-start.6

commit v3 on v2

--- a/solution.py
+++ b/solution.py
@@ -33,7 +33,7 @@
     return jnp.concatenate([square] * (columns // LANES), axis=1)
 
 
-def arrival_order(piece=2.2, latency=1.6, ahead=3):
+def arrival_order(piece=1.1, latency=1.6, ahead=4):
     free = dict.fromkeys("UDRL", 0.0)
     now = 0.0
     pending = {}
@@ -59,7 +59,7 @@
         across(0, s)
     following = ahead
     count = [0] * DP_Z
-    tasks = [(0.0, "tstat", 2.0), (8.0, "tables", 1.5), (9.0, "text2", 0.3), (20.0, "text3", 2.5)]
+    tasks = []
     while pending or tasks:
         here = [k for k, t in pending.items() if t <= now]
         ready = [t for t in tasks if t[0] <= now]
@@ -153,6 +153,7 @@
     or_sem,
     as_sem,
     ar_sem,
+    turn_sem,
 ):
     groups, ranks, features = dims
     grp = lax.axis_index("grp")
@@ -341,8 +342,6 @@
         values = jnp.where(slot == 3, last, values)
         table[...] = values
         table_smem.start()
-        place_own.start()
-        to_groups(table_copy, start)
 
     def table_copy(peer):
         return remote(table.at[peer], places_ref.at[grp], os_sem.at[peer], or_sem.at[grp], grp=peer)
@@ -386,10 +385,21 @@
     table_smem = pltpu.make_async_copy(table, table_s, local_sem.at[1])
     place_own = pltpu.make_async_copy(table.at[grp], places_ref.at[grp], local_sem.at[2])
     out_own = pltpu.make_async_copy(outbox.at[grp], arrived_ref.at[grp], local_sem.at[3])
-    work = {"tstat": text_first, "tables": tables, "text2": text_second, "text3": text_third}
+
+    @pl.when(core == 1)
+    def _():
+        pl.semaphore_wait(turn_sem, 1)
 
     opened = False
-    for step in arrival_order():
+    order = arrival_order()
+    handover = 1 + max(n for n, step in enumerate(order) if step[0] == "z" and step[2] <= 1)
+    for n, step in enumerate(order):
+        if n == handover:
+
+            @pl.when(core == 0)
+            def _():
+                pl.semaphore_signal(turn_sem, inc=1, device_id={"grp": grp + 1 - 2 * core}, device_id_type=MESH)
+
         if step[0] == "own":
             for d in "UD":
                 go(z_copy(d, 1, step[1]))
@@ -398,13 +408,10 @@
             if step[1] == PIECES - 1:
                 to_ranks(start)
         elif step[0] == "task":
-            if step[1] in work:
-                work[step[1]]()
-            else:
-                if not opened:
-                    loads[8].wait()
-                    opened = True
-                project(step[1])
+            if not opened:
+                loads[8].wait()
+                opened = True
+            project(step[1])
         elif step[0] == "z":
             _, d, age, s = step
             z_arrival(d, age, s).wait_recv()
@@ -420,9 +427,10 @@
                 go(x_copy(q, source, d, s, xr_sem.at[q, s]))
 
     stats_start(x_stats, pstat_x, ps_sem, pr_sem)
-    table_smem.wait()
+    tables()
     pstat_z[zi] = stats_sum(x_stats, pstat_x, ps_sem, pr_sem)
     stats_start(z_stats, pstat_z, ps_sem, pr_sem)
+    table_smem.wait()
     for k in range(1, 4):
         z_stats(pstat_z, ps_sem, pr_sem, k, False).wait_recv()
 
@@ -444,6 +452,12 @@
 
     to_groups(out_copy, start)
     out_own.start()
+    place_own.start()
+    to_groups(table_copy, start)
+
+    text_first()
+    text_second()
+    text_third()
 
     to_ranks(wait_send)
     to_groups(table_copy, wait_send)
@@ -465,10 +479,20 @@
     out_own.wait()
 
 
-def overlay_kernel(places_ref, thid_ref, arrived_ref, out_ref, rows):
+def overlay_kernel(places_hbm, thid_hbm, arrived_hbm, out_hbm, places_ref, thid_ref, arrived_ref, rows, sem):
     chunks = rows.shape[0]
-    for c in range(chunks):
-        rows[c] = thid_ref[:, c * LANES : (c + 1) * LANES].astype(jnp.float32)
+    blocks = thid_ref.shape[0]
+    places_copy = pltpu.make_async_copy(places_hbm, places_ref, sem.at[0])
+    arrived_copy = pltpu.make_async_copy(arrived_hbm, arrived_ref, sem.at[1])
+    loads = [pltpu.make_async_copy(thid_hbm.at[b], thid_ref.at[b], sem.at[2 + b]) for b in range(blocks)]
+    for copy in [places_copy, *loads, arrived_copy]:
+        copy.start()
+    for b in range(blocks):
+        loads[b].wait()
+        for c in range(chunks):
+            rows[c, b * LANES : (b + 1) * LANES] = thid_ref[b, :, c * LANES : (c + 1) * LANES].astype(jnp.float32)
+    places_copy.wait()
+    arrived_copy.wait()
 
     @pl.loop(0, arrived_ref.shape[0])
     def _(g):
@@ -481,8 +505,15 @@
                 for c in range(chunks):
                     rows[c, pl.ds(at, PATCH), :] = image[:, c * LANES : (c + 1) * LANES]
 
-    for c in range(chunks):
-        out_ref[:, c * LANES : (c + 1) * LANES] = rows[c].astype(jnp.bfloat16)
+    stores = []
+    for b in range(blocks):
+        for c in range(chunks):
+            thid_ref[b, :, c * LANES : (c + 1) * LANES] = rows[c, b * LANES : (b + 1) * LANES].astype(jnp.bfloat16)
+        copy = pltpu.make_async_copy(thid_ref.at[b], out_hbm.at[b], sem.at[2 + b])
+        copy.start()
+        stores.append(copy)
+    for copy in stores:
+        copy.wait()
 
 
 def on_device(
@@ -504,8 +535,6 @@
     text_blocks = seq_len // LANES
     stat_blocks = slots * PATCH // LANES
     bf16, f32, i32 = jnp.bfloat16, jnp.float32, jnp.int32
-    vmem = pl.BlockSpec(memory_space=pltpu.VMEM)
-    smem = pl.BlockSpec(memory_space=pltpu.SMEM)
     hbm = pl.BlockSpec(memory_space=pltpu.HBM)
     dma = pltpu.SemaphoreType.DMA
     arrived, places, thid = pl.pallas_call(
@@ -555,9 +584,10 @@
             dma((groups,)),
             dma((groups,)),
             dma((groups,)),
+            pltpu.SemaphoreType.REGULAR,
         ],
         compiler_params=pltpu.CompilerParams(
-            collective_id=0, has_side_effects=True, vmem_limit_bytes=48 << 20
+            collective_id=0, has_side_effects=True, vmem_limit_bytes=60 << 20
         ),
         name="exchange",
     )(
@@ -571,15 +601,22 @@
         owner_block,
         offsets,
     )
-    return pl.pallas_call(
+    hidden = pl.pallas_call(
         overlay_kernel,
-        out_shape=jax.ShapeDtypeStruct((seq_len, columns), bf16),
-        in_specs=[smem, vmem, vmem],
-        out_specs=vmem,
-        scratch_shapes=[pltpu.VMEM((columns // LANES, seq_len, LANES), f32)],
-        compiler_params=pltpu.CompilerParams(vmem_limit_bytes=32 << 20),
+        out_shape=jax.ShapeDtypeStruct((text_blocks, LANES, columns), bf16),
+        in_specs=[hbm] * 3,
+        out_specs=pl.BlockSpec(memory_space=pl.ANY),
+        scratch_shapes=[
+            pltpu.SMEM((groups, 1, LANES), i32),
+            pltpu.VMEM((text_blocks, LANES, columns), bf16),
+            pltpu.VMEM((groups, CAP, PATCH, columns), bf16),
+            pltpu.VMEM((columns // LANES, seq_len, LANES), f32),
+            dma((2 + text_blocks,)),
+        ],
+        compiler_params=pltpu.CompilerParams(vmem_limit_bytes=60 << 20),
         name="overlay",
-    )(places, thid.reshape(seq_len, columns), arrived)
+    )(places, thid, arrived)
+    return hidden.reshape(seq_len, columns)
 
 
 def solution(mesh):

time: 149 us -> 142 us (0.953)
  the two profiles are of different devices: /device:TPU:279 before, /device:TPU:97 now
where the time goes in v3:
time: 142 us; the launch traced here: 141 us
  Pallas kernels  141 us (99%)
    pallas_call x1, Pallas kernels, on_device(): pl.pallas_call(functools.partial(exchange_kernel, (groups, ranks, ranks *...  136 us
    pallas_call x1, Pallas kernels, on_device(): pl.pallas_call(overlay_kernel, out_shape=jax.ShapeDtypeStruct((text_block...  4.32 us

profile of v3, /device:TPU:97, one launch (start us, length us, event | category | flops | bytes accessed | tf_op | source)
XLA Modules:
  0.0 141.4 jit_solution(3241074940759330655)
XLA Ops:
  0.7 136.4 %exchange.1 = (bf16[48,2,16,512]{3,2,1,0:T(8,128)(2,1)}, s32[48,1,128]{2,1,0:T(1,128)}, bf16[12,128,512]{2,1,0:T(8,128)(2,1)}) custom-call(bf16[64,3200]{1,0:T(8,128)(2,1)} %vis_hbm.1, f32[3200]{0:T(1024)} %vgain_hbm.1, bf16[3200,512]{1,0:T(8,128)(2,1)} %w_hbm.1, f32[512]{0:T(512)} %bias_hbm.1, bf16[12,128,512]{2,1,0:T(8,128)(2,1)} %bitcast.2, ...), custom_call_target="tpu_custom_call" | custom-call | tf_op jit(solution)/shard_map/exchange/pallas_call | solution.py:540
  137.1 4.3 %overlay.1 = bf16[12,128,512]{2,1,0:T(8,128)(2,1)} custom-call(s32[48,1,128]{2,1,0:T(1,128)} %get-tuple-element.8.places_hbm, bf16[12,128,512]{2,1,0:T(8,128)(2,1)} %get-tuple-element.9.thid_hbm, bf16[48,2,16,512]{3,2,1,0:T(8,128)(2,1)} %get-tuple-element.10.arrived_hbm), custom_call_target="tpu_custom_call" | custom-call | tf_op jit(solution)/shard_map/overlay/pallas_call | solution.py:604

commit v4 on v3

--- a/solution.py
+++ b/solution.py
@@ -392,7 +392,7 @@
 
     opened = False
     order = arrival_order()
-    handover = 1 + max(n for n, step in enumerate(order) if step[0] == "z" and step[2] <= 1)
+    handover = 1 + max(n for n, step in enumerate(order) if step[0] == "z" and (step[2] <= 2 or step[2:] in ((3, 0), (3, 1))))
     for n, step in enumerate(order):
         if n == handover:
 
@@ -450,7 +450,14 @@
         for r in range(CAP):
             outbox[o, r] = proj[table_s[o, 0, CAP + r]]
 
-    to_groups(out_copy, start)
+    @pl.loop(0, groups // 2)
+    def _(k):
+        out_copy((grp + 1 + k) % groups).start()
+
+        @pl.when(k < groups // 2 - 1)
+        def _():
+            out_copy((grp + groups - 1 - k) % groups).start()
+
     out_own.start()
     place_own.start()
     to_groups(table_copy, start)

time: 142 us -> 134 us (0.944)
  the two profiles are of different devices: /device:TPU:97 before, /device:TPU:65 now
where the time goes in v4:
time: 134 us
  Pallas kernels  133 us (99%)
    pallas_call x1, Pallas kernels, on_device(): pl.pallas_call(functools.partial(exchange_kernel, (groups, ranks, ranks *...  129 us
    pallas_call x1, Pallas kernels, on_device(): pl.pallas_call(overlay_kernel, out_shape=jax.ShapeDtypeStruct((text_block...  4.32 us

profile of v4, /device:TPU:65, one launch (start us, length us, event | category | flops | bytes accessed | tf_op | source)
XLA Modules:
  0.0 134.1 jit_solution(7687740473548261645)
XLA Ops:
  0.7 129.2 %exchange.1 = (bf16[48,2,16,512]{3,2,1,0:T(8,128)(2,1)}, s32[48,1,128]{2,1,0:T(1,128)}, bf16[12,128,512]{2,1,0:T(8,128)(2,1)}) custom-call(bf16[64,3200]{1,0:T(8,128)(2,1)} %vis_hbm.1, f32[3200]{0:T(1024)} %vgain_hbm.1, bf16[3200,512]{1,0:T(8,128)(2,1)} %w_hbm.1, f32[512]{0:T(512)} %bias_hbm.1, bf16[12,128,512]{2,1,0:T(8,128)(2,1)} %bitcast.2, ...), custom_call_target="tpu_custom_call" | custom-call | tf_op jit(solution)/shard_map/exchange/pallas_call | solution.py:547
  129.8 4.3 %overlay.1 = bf16[12,128,512]{2,1,0:T(8,128)(2,1)} custom-call(s32[48,1,128]{2,1,0:T(1,128)} %get-tuple-element.8.places_hbm, bf16[12,128,512]{2,1,0:T(8,128)(2,1)} %get-tuple-element.9.thid_hbm, bf16[48,2,16,512]{3,2,1,0:T(8,128)(2,1)} %get-tuple-element.10.arrived_hbm), custom_call_target="tpu_custom_call" | custom-call | tf_op jit(solution)/shard_map/overlay/pallas_call | solution.py:611
